TPU v7x, 32 devices: a whole 2x2x4 slice. The times are simulated.
32 devices in a mesh: batch: 16 (over z, y, x), mp: 2 (over core).
Axes of the slice: x: 2, y: 2, z: 4, core: 2. Of those that a mesh axis runs over, the one named last changes fastest.
Arguments:
- hidden: bfloat16 [16384, 1024], P(('batch', 'mp')), may hold values from -6 to 6
- cell_ids: int32 [32, 512], P('batch'), may hold values from 0 to 127, never falling along the last dimension, each value on 1 to 60 neighbouring positions
- boxes: int32 [32, 128, 4], P('batch'), may hold values from 0 to 1023
- x_table: bfloat16 [1024, 1024], replicated, may hold values from -3 to 3
- y_table: bfloat16 [1024, 1024], replicated, may hold values from -3 to 3
- w_query: bfloat16 [1024, 1024], P(None, 'mp'), may hold values from -0.1875 to 0.1875
- b_query: bfloat16 [1024], P('mp'), may hold values from -3 to 3
- w_key: bfloat16 [1024, 1024], P(None, 'mp'), may hold values from -0.1875 to 0.1875
- w_value: bfloat16 [1024, 1024], P(None, 'mp'), may hold values from -0.1875 to 0.1875
- b_value: bfloat16 [1024], P('mp'), may hold values from -3 to 3
- w_out: bfloat16 [1024, 1024], P('mp'), may hold values from -3 to 3
- b_out: bfloat16 [1024], replicated, may hold values from -3 to 3
- ln1_gain: bfloat16 [1024], replicated, may hold values from 0.5 to 1.5
- ln1_bias: bfloat16 [1024], replicated, may hold values from -1 to 1
- w_up: bfloat16 [1024, 4096], P(None, 'mp'), may hold values from -0.1875 to 0.1875
- b_up: bfloat16 [4096], P('mp'), may hold values from -3 to 3
- w_down: bfloat16 [4096, 1024], P('mp'), may hold values from -0.09375 to 0.09375
- b_down: bfloat16 [1024], replicated, may hold values from -3 to 3
- ln2_gain: bfloat16 [1024], replicated, may hold values from 0.5 to 1.5
- ln2_bias: bfloat16 [1024], replicated, may hold values from -1 to 1
- d_out: bfloat16 [16384, 1024], P(('batch', 'mp')), may hold values from -6 to 6
Outputs:
- layer_out: bfloat16 [16384, 1024], P(('batch', 'mp'))
- d_hidden: float32 [16384, 1024], P(('batch', 'mp'))
- grad_w_query: float32 [1024, 1024], P(None, 'mp')
- grad_b_query: float32 [1024], P('mp')
- grad_w_key: float32 [1024, 1024], P(None, 'mp')
- grad_w_value: float32 [1024, 1024], P(None, 'mp')
- grad_b_value: float32 [1024], P('mp')
- grad_w_out: float32 [1024, 1024], P('mp')
- grad_b_out: float32 [1024], replicated
- grad_ln1_gain: float32 [1024], replicated
- grad_ln1_bias: float32 [1024], replicated
- grad_w_up: float32 [1024, 4096], P(None, 'mp')
- grad_b_up: float32 [4096], P('mp')
- grad_w_down: float32 [4096, 1024], P('mp')
- grad_b_down: float32 [1024], replicated
- grad_ln2_gain: float32 [1024], replicated
- grad_ln2_bias: float32 [1024], replicated
Inputs may be any that keep to these rules, and one draw needn't show every extreme that they name: `cell_ids`: numbered from 0 within each page, never falling along a page; each of the 128 cells has 1 to 60 tokens and one has 60.
All inputs are finite; a program needn't handle non-finite values.
Results may differ from a plain program's by a relative error of at most 0.023.
Values may be sent and summed in bfloat16 or wider, within the bound.
No kernel may reach another device: no remote copies, remote signals or barrier semaphores. Data moves between devices by JAX's collectives and lax.ppermute only.
A program may use at most 128 MiB of HBM per device.

v0:
```python
import jax
import jax.numpy as jnp
from jax import lax
from jax.sharding import PartitionSpec as P

HDIM = 64
PAGE_LEN = 512
CELLS = 128


def contract_rows(left, right):
    return lax.dot_general(
        left, right, (((0,), (0,)), ((), ())), preferred_element_type=jnp.float32
    )


def contract_last(left, right):
    return lax.dot_general(
        left, right, (((1,), (1,)), ((), ())), preferred_element_type=jnp.float32
    )


def layer_norm(values, gain, shift):
    average = jnp.mean(values, axis=-1, keepdims=True)
    centred = values - average
    rstd_rows = lax.rsqrt(jnp.mean(centred * centred, axis=-1, keepdims=True) + 1e-12)
    normed = centred * rstd_rows
    return (normed * gain + shift, normed, rstd_rows)


def norm_back(upstream, normed, rstd_rows, gain):
    scaled = upstream * gain
    return rstd_rows * (
        scaled
        - jnp.mean(scaled, axis=-1, keepdims=True)
        - normed * jnp.mean(scaled * normed, axis=-1, keepdims=True)
    )


def gelu_slope(values):
    return (
        0.5 * (1.0 + lax.erf(values * 0.7071067811865476))
        + values * jnp.exp(-0.5 * values * values) * 0.3989422804014327
    )


def page_scores(queries, keys_page):
    return jnp.einsum(
        "qhd,khd->hqk", queries, keys_page, preferred_element_type=jnp.float32
    ) * HDIM ** (-0.5)


def attend(page_block):
    queries, keys_page, values_page = page_block
    scores = page_scores(queries, keys_page)
    maximum = jnp.max(scores, axis=-1, keepdims=True)
    log_total = maximum + jnp.log(jnp.sum(jnp.exp(scores - maximum), axis=-1, keepdims=True))
    weights = jnp.exp(scores - log_total).astype(jnp.bfloat16)
    context = jnp.einsum("hqk,khd->qhd", weights, values_page, preferred_element_type=jnp.float32)
    return (context.astype(jnp.bfloat16), log_total[..., 0])


def attend_back(page_block):
    queries, keys_page, values_page, log_total, d_context = page_block
    weights = jnp.exp(page_scores(queries, keys_page) - log_total[..., None])
    d_weights = jnp.einsum(
        "qhd,khd->hqk", d_context, values_page, preferred_element_type=jnp.float32
    )
    d_values = jnp.einsum(
        "hqk,qhd->khd", weights.astype(jnp.bfloat16), d_context, preferred_element_type=jnp.float32
    )
    d_scores = (
        weights * (d_weights - jnp.sum(weights * d_weights, axis=-1, keepdims=True))
    ).astype(jnp.bfloat16)
    factor = HDIM ** (-0.5)
    d_queries = (
        jnp.einsum("hqk,khd->qhd", d_scores, keys_page, preferred_element_type=jnp.float32) * factor
    )
    d_keys = (
        jnp.einsum("hqk,qhd->khd", d_scores, queries, preferred_element_type=jnp.float32) * factor
    )
    return (
        d_queries.astype(jnp.bfloat16),
        d_keys.astype(jnp.bfloat16),
        d_values.astype(jnp.bfloat16),
    )


def shards(
    hidden,
    cell_ids,
    boxes,
    x_table,
    y_table,
    w_query,
    b_query,
    w_key,
    w_value,
    b_value,
    w_out,
    b_out,
    ln1_gain,
    ln1_bias,
    w_up,
    b_up,
    w_down,
    b_down,
    ln2_gain,
    ln2_bias,
    d_out,
):
    row_count = hidden.shape[0]
    width_local = w_query.shape[1]
    first_row = lax.axis_index("mp") * row_count
    own_cells = lax.dynamic_slice_in_dim(cell_ids.reshape(-1), first_row, row_count)
    page_local = (first_row + jnp.arange(row_count, dtype=jnp.int32)) // PAGE_LEN
    cell_boxes = jnp.take(boxes.reshape(-1, 4), page_local * CELLS + own_cells, axis=0)
    layout = (
        jnp.take(x_table, cell_boxes[:, 0], axis=0).astype(jnp.float32)
        + jnp.take(y_table, cell_boxes[:, 1], axis=0).astype(jnp.float32)
        + jnp.take(x_table, cell_boxes[:, 2], axis=0).astype(jnp.float32)
        + jnp.take(y_table, cell_boxes[:, 3], axis=0).astype(jnp.float32)
    )
    inputs = hidden.astype(jnp.float32) + layout
    x_all = lax.all_gather(inputs.astype(jnp.bfloat16), "mp", axis=0, tiled=True)
    queries = (
        jnp.dot(x_all, w_query, preferred_element_type=jnp.float32) + b_query.astype(jnp.float32)
    ).astype(jnp.bfloat16)
    keys_all = jnp.dot(x_all, w_key, preferred_element_type=jnp.float32).astype(jnp.bfloat16)
    values_all = (
        jnp.dot(x_all, w_value, preferred_element_type=jnp.float32) + b_value.astype(jnp.float32)
    ).astype(jnp.bfloat16)
    page_shape = (-1, PAGE_LEN, width_local // HDIM, HDIM)
    page_split = (
        queries.reshape(page_shape),
        keys_all.reshape(page_shape),
        values_all.reshape(page_shape),
    )
    context, log_total = lax.map(attend, page_split)
    context = context.reshape(-1, width_local)
    attn_rows = lax.psum_scatter(
        jnp.dot(context, w_out, preferred_element_type=jnp.float32),
        "mp",
        scatter_dimension=0,
        tiled=True,
    )
    resid = inputs + attn_rows + b_out.astype(jnp.float32)
    hidden_mid, normed_one, rstd_one = layer_norm(
        resid, ln1_gain.astype(jnp.float32), ln1_bias.astype(jnp.float32)
    )
    mid_low = hidden_mid.astype(jnp.bfloat16)
    mid_all = lax.all_gather(mid_low, "mp", axis=0, tiled=True)
    pre_act = jnp.dot(mid_all, w_up, preferred_element_type=jnp.float32) + b_up.astype(jnp.float32)
    activ = jax.nn.gelu(pre_act, approximate=False).astype(jnp.bfloat16)
    ffn_rows = lax.psum_scatter(
        jnp.dot(activ, w_down, preferred_element_type=jnp.float32),
        "mp",
        scatter_dimension=0,
        tiled=True,
    )
    second = hidden_mid + ffn_rows + b_down.astype(jnp.float32)
    final, normed_two, rstd_two = layer_norm(
        second, ln2_gain.astype(jnp.float32), ln2_bias.astype(jnp.float32)
    )
    layer_out = final.astype(jnp.bfloat16)
    upstream = d_out.astype(jnp.float32)
    grad_ln2_gain = jnp.sum(upstream * normed_two, axis=0)
    grad_ln2_bias = jnp.sum(upstream, axis=0)
    d_second = norm_back(upstream, normed_two, rstd_two, ln2_gain.astype(jnp.float32))
    grad_b_down = jnp.sum(d_second, axis=0)
    second_low = d_second.astype(jnp.bfloat16)
    grads_all = lax.all_gather(second_low, "mp", axis=0, tiled=True)
    grad_w_down = contract_rows(activ, grads_all)
    d_pre = (contract_last(grads_all, w_down) * gelu_slope(pre_act)).astype(jnp.bfloat16)
    grad_w_up = contract_rows(mid_all, d_pre)
    grad_b_up = jnp.sum(d_pre.astype(jnp.float32), axis=0)
    d_mid_ffn = lax.psum_scatter(contract_last(d_pre, w_up), "mp", scatter_dimension=0, tiled=True)
    d_mid = d_second + d_mid_ffn
    grad_ln1_gain = jnp.sum(d_mid * normed_one, axis=0)
    grad_ln1_bias = jnp.sum(d_mid, axis=0)
    d_resid = norm_back(d_mid, normed_one, rstd_one, ln1_gain.astype(jnp.float32))
    grad_b_out = jnp.sum(d_resid, axis=0)
    resid_all = lax.all_gather(d_resid.astype(jnp.bfloat16), "mp", axis=0, tiled=True)
    grad_w_out = contract_rows(context, resid_all)
    d_context = contract_last(resid_all, w_out).astype(jnp.bfloat16).reshape(page_shape)
    d_queries, d_keys, d_values = lax.map(attend_back, page_split + (log_total, d_context))
    d_queries = d_queries.reshape(-1, width_local)
    d_keys = d_keys.reshape(-1, width_local)
    d_values = d_values.reshape(-1, width_local)
    grad_w_query = contract_rows(x_all, d_queries)
    grad_w_key = contract_rows(x_all, d_keys)
    grad_w_value = contract_rows(x_all, d_values)
    grad_b_query = jnp.sum(d_queries.astype(jnp.float32), axis=0)
    grad_b_value = jnp.sum(d_values.astype(jnp.float32), axis=0)
    d_hidden = d_resid + lax.psum_scatter(
        (
            contract_last(d_queries, w_query)
            + contract_last(d_keys, w_key)
            + contract_last(d_values, w_value)
        ).astype(jnp.bfloat16),
        "mp",
        scatter_dimension=0,
        tiled=True,
    ).astype(jnp.float32)
    (
        grad_w_query,
        grad_b_query,
        grad_w_key,
        grad_w_value,
        grad_b_value,
        grad_w_out,
        grad_w_up,
        grad_b_up,
        grad_w_down,
    ) = (
        lax.psum(grad_w_query.astype(jnp.bfloat16), "batch").astype(jnp.float32),
        lax.psum(grad_b_query.astype(jnp.bfloat16), "batch").astype(jnp.float32),
        lax.psum(grad_w_key.astype(jnp.bfloat16), "batch").astype(jnp.float32),
        lax.psum(grad_w_value.astype(jnp.bfloat16), "batch").astype(jnp.float32),
        lax.psum(grad_b_value.astype(jnp.bfloat16), "batch").astype(jnp.float32),
        lax.psum(grad_w_out.astype(jnp.bfloat16), "batch").astype(jnp.float32),
        lax.psum(grad_w_up.astype(jnp.bfloat16), "batch").astype(jnp.float32),
        lax.psum(grad_b_up.astype(jnp.bfloat16), "batch").astype(jnp.float32),
        lax.psum(grad_w_down.astype(jnp.bfloat16), "batch").astype(jnp.float32),
    )
    grad_b_out, grad_ln1_gain, grad_ln1_bias, grad_b_down, grad_ln2_gain, grad_ln2_bias = lax.psum(
        (grad_b_out, grad_ln1_gain, grad_ln1_bias, grad_b_down, grad_ln2_gain, grad_ln2_bias),
        ("batch", "mp"),
    )
    return (
        layer_out,
        d_hidden,
        grad_w_query,
        grad_b_query,
        grad_w_key,
        grad_w_value,
        grad_b_value,
        grad_w_out,
        grad_b_out,
        grad_ln1_gain,
        grad_ln1_bias,
        grad_w_up,
        grad_b_up,
        grad_w_down,
        grad_b_down,
        grad_ln2_gain,
        grad_ln2_bias,
    )


def solution(mesh):
    in_specs = (
        P(("batch", "mp"), None),
        P("batch", None),
        P("batch", None, None),
        P(),
        P(),
        P(None, "mp"),
        P("mp"),
        P(None, "mp"),
        P(None, "mp"),
        P("mp"),
        P("mp", None),
        P(),
        P(),
        P(),
        P(None, "mp"),
        P("mp"),
        P("mp", None),
        P(),
        P(),
        P(),
        P(("batch", "mp"), None),
    )
    out_specs = (
        P(("batch", "mp"), None),
        P(("batch", "mp"), None),
        P(None, "mp"),
        P("mp"),
        P(None, "mp"),
        P(None, "mp"),
        P("mp"),
        P("mp", None),
        P(),
        P(),
        P(),
        P(None, "mp"),
        P("mp"),
        P("mp", None),
        P(),
        P(),
        P(),
    )
    return jax.shard_map(shards, mesh=mesh, in_specs=in_specs, out_specs=out_specs, check_vma=False)
```

profile of v0, /device:TPU:0, one launch (start us, length us, event | category | flops | bytes accessed | tf_op | source)
XLA Modules:
  0.0 700.1 jit_solution(8458839634089925012)
XLA Ops:
  12.9 2.8 gather_fusion.3
  15.7 5.5 gather_fusion.2
  21.2 2.8 gather_fusion.4
  24.0 4.1 fusion.92
  28.2 13.3 %all-gather.5.cloned.1.call-done = bf16[1024,1024]{1,0:T(8,128)(2,1)} async-done(((bf16[512,1024]{1,0:T(8,128)(2,1)}), bf16[1024,1024]{1,0:T(8,128)(2,1)}) %all-gather.5.cloned.1.call-update) | async-done | bytes 2097168 | tf_op jit(solution)/shard_map/all_gather | solution.py:125
  41.5 2.8 add_convert_fusion.3
  44.4 2.4 reshape.218
  46.7 2.5 copy.58
  49.2 3.1 add_convert_fusion.2
  54.4 2.5 copy.59
  56.9 3.1 convolution_convert_fusion.7
  62.1 2.5 copy.60
  65.7 10.6 %while.26 = (s32[]{:T(128)}, bf16[2,512,8,64]{1,3,2,0:T(8,128)(2,1)}, f32[2,8,512]{2,1,0:T(8,128)S(1)}, bf16[2,512,8,64]{1,3,2,0:T(8,128)(2,1)S(1)}, bf16[2,512,...) while((s32[]{:T(128)}, bf16[2,512,8,64]{1,3,2,0:T(8,128)(2,1)}, ...), condition=%wide.region_3.5_spmd, body=%wide.region_0.4_spmd.sunk | while | flops 553906176 | bytes 35784840 | solution.py:139
  76.3 3.2 copy.61
  80.8 3.3 fusion.94
  84.8 12.7 %reduce-scatter.5.cloned.1.call-done = f32[512,1024]{1,0:T(8,128)} async-done(((f32[1024,1024]{1,0:T(8,128)}), f32[512,1024]{1,0:T(8,128)}) %reduce-scatter.5.cloned.1.call-update) | async-done | bytes 2097168 | tf_op jit(solution)/shard_map/reduce_scatter | solution.py:141
  97.5 2.5 fusion.91
  101.9 12.0 %all-gather.7.cloned.1.call-done = bf16[1024,1024]{1,0:T(8,128)(2,1)} async-done(((bf16[512,1024]{1,0:T(8,128)(2,1)}), bf16[1024,1024]{1,0:T(8,128)(2,1)}) %all-gather.7.cloned.1.call-update) | async-done | bytes 2097168 | tf_op jit(solution)/shard_map/all_gather | solution.py:152
  113.8 25.3 %fusion.60 = (bf16[1024,2048]{1,0:T(8,128)(2,1)S(1)}, f32[1024,2048]{1,0:T(8,128)}) fusion(f32[2048]{0:T(1024)S(1)} %convert_element_type.185, bf16[1024,1024]{1,0:T(8,128)(2,1)} %all-gather.7.cloned.1.call-done, bf16[1024,2048]{1,0:T(8,128)(2,1)} %param.41), kind=kOutput, calls=%fused_computation.71 | convolution fusion | flops 4433379328 | bytes 18882560 | tf_op jit(solution)/shard_map/dot_general | solution.py:153
  141.1 6.0 fusion.95
  147.8 12.7 %reduce-scatter.7.cloned.1.call-done = f32[512,1024]{1,0:T(8,128)} async-done(((f32[1024,1024]{1,0:T(8,128)}), f32[512,1024]{1,0:T(8,128)}) %reduce-scatter.7.cloned.1.call-update) | async-done | bytes 2097168 | tf_op jit(solution)/shard_map/reduce_scatter | solution.py:155
  160.5 2.3 fusion.90
  164.8 2.4 fusion.87
  169.9 11.8 %all-gather.9.cloned.1.call-done = bf16[1024,1024]{1,0:T(8,128)(2,1)} async-done(((bf16[512,1024]{1,0:T(8,128)(2,1)}), bf16[1024,1024]{1,0:T(8,128)(2,1)}) %all-gather.9.cloned.1.call-update) | async-done | bytes 2097168 | tf_op jit(solution)/shard_map/all_gather | solution.py:172
  181.7 11.5 %fusion.93 = (bf16[2048]{0:T(1024)(128)(2,1)}, bf16[1024,2048]{1,0:T(8,128)(2,1)S(1)}) fusion(f32[1024,2048]{1,0:T(8,128)} %get-tuple-element.213, f32[2048]{0:T(1024)S(1)} %convert_element_type.185, bf16[1024,1024]{1,0:T(8,128)(2,1)} %all-gather.9.cloned.1.call-done, bf16[2048,1024]{1,0:T(8,128)(2,1)} %param.43), kind=kOutput, calls=%fused_computation.173 | convolution fusion | flops 4320131072 | bytes 18886656 | tf_op jit(solution)/shard_map/dot_general | solution.py:18
  195.2 6.1 fusion.96
  201.3 13.3 %reduce-scatter.9.cloned.1.call-done = f32[512,1024]{1,0:T(8,128)} async-done(((f32[1024,1024]{1,0:T(8,128)}), f32[512,1024]{1,0:T(8,128)}) %reduce-scatter.9.cloned.1.call-update) | async-done | bytes 2097168 | tf_op jit(solution)/shard_map/reduce_scatter | solution.py:177
  214.6 3.2 multiply_reduce_fusion.2
  221.2 11.8 %all-gather.11.cloned.1.call-done = bf16[1024,1024]{1,0:T(8,128)(2,1)} async-done(((bf16[512,1024]{1,0:T(8,128)(2,1)}), bf16[1024,1024]{1,0:T(8,128)(2,1)}) %all-gather.11.cloned.1.call-update) | async-done | bytes 2097168 | tf_op jit(solution)/shard_map/all_gather | solution.py:183
  233.0 3.8 convolution_convert_fusion.6
  236.9 4.0 reshape.217
  240.9 3.3 copy.65
  247.4 23.9 %while.27 = (s32[]{:T(128)}, bf16[2,512,8,64]{1,3,2,0:T(8,128)(2,1)}, bf16[2,512,8,64]{1,3,2,0:T(8,128)(2,1)}, bf16[2,512,8,64]{1,3,2,0:T(8,128)(2,1)}, bf16[2,5...) while((s32[]{:T(128)}, ...), condition=%wide.region_17.19_spmd, body=%wide.region_15.18_spmd.sunk | while | flops 1368649728 | bytes 89249008 | solution.py:186
  251.1 2.6 multiply_convert_fusion.2
  256.9 2.4 fusion.164
  262.9 2.6 multiply_convert_fusion.2
  268.7 2.4 fusion.164
  271.4 2.5 copy.69
  279.7 2.7 add_convert_fusion
  283.0 9.5 %convolution_convert_fusion = bf16[2048,1024]{1,0:T(8,128)(2,1)} fusion(bf16[1024,2048]{1,0:T(8,128)(2,1)} %copy-done.61, bf16[1024,1024]{1,0:T(8,128)(2,1)} %all-gather.9.cloned.1.call-done), kind=kOutput, calls=%fused_computation.94 | convolution fusion | flops 4297064448 | bytes 10485760 | tf_op jit(solution)/shard_map/dot_general | solution.py:12
  292.5 6.2 convolution_convert_fusion.1
  298.8 2.3 convolution_convert_fusion.2
  308.7 44.8 %all-reduce = (f32[1024]{0:T(1024)}, f32[1024]{0:T(1024)}, f32[1024]{0:T(1024)}, f32[1024]{0:T(1024)}, f32[1024]{0:T(1024)}, /*index=5*/f32[1024]{0:T(1024)}) all-reduce(f32[1024]{0:T(1024)S(1)} %get-tuple-element.196, f32[1024]{0:T(1024)S(1)} %get-tuple-element.135, ...), channel_id=1, replica_groups=mesh['batch'=16,'mp'=2] {'batch','mp'}, use_global_device_ids=true, to_apply=%region_28.30 | all-reduce | flops 6144 | bytes 49152 | tf_op jit(solution)/shard_map/psum | solution.py:226
  355.3 44.0 %all-reduce.1 = (bf16[512]{0:T(512)(128)(2,1)S(1)}, bf16[512]{0:T(512)(128)(2,1)S(1)}, bf16[2048]{0:T(1024)(128)(2,1)S(1)}) all-reduce(bf16[512]{0:T(512)(128)(2,1)S(1)} %reduce_sum.193, bf16[512]{0:T(512)(128)(2,1)S(1)} %reduce_sum.195, bf16[2048]{0:T(1024)(128)(2,1)S(1)} %copy-done.43), channel_id=1, replica_groups=mesh['batch'=16,'mp'=2] {'batch'}, use_global_device_ids=true, to_apply=%region_21.23 | all-reduce | flops 3072 | bytes 12288 | tf_op jit(solution)/shard_map/psum | solution.py:217
  401.1 3.0 convert_add_fusion
  404.0 271.6 %all-reduce.5.cloned.1.call-done = (bf16[1024,512]{1,0:T(8,128)(2,1)}, bf16[1024,512]{1,0:T(8,128)(2,1)}, bf16[1024,512]{1,0:T(8,128)(2,1)}, bf16[512,1024]{1,0:...) async-done(((bf16[1024,512]{1,0:T(8,128)(2,1)}, bf16[1024,512]{1,0:T(8,128)(2,1)}, bf16[1024,512]{1,0:T(8,128)(2,1)}, bf16[512,1024]{1,0:T(8,128)(2,1)}, ...) | async-done | bytes 12582928 | tf_op jit(solution)/shard_map/psum | solution.py:216
  675.7 6.8 convert_element_type.209
  682.5 4.4 convert_element_type.212
  (244 shorter events, 78.6 us)
Async XLA Ops:
  7.2 3.7 copy-start
  7.2 34.3 %all-gather.5.cloned.1.call-start = ((), (), s32[]{:S(2)}) async-start(), calls=%async_computation.4 | async-start | bytes 3145728 | tf_op jit(solution)/shard_map/all_gather | solution.py:125
  15.7 5.5 copy-start.2
  24.0 4.2 copy-start.50
  24.0 4.2 copy-start.51
  24.0 17.5 %copy-start.25 = (bf16[1024,512]{1,0:T(8,128)(2,1)S(1)}, bf16[1024,512]{1,0:T(8,128)(2,1)}, u32[]{:S(2)}) copy-start(bf16[1024,512]{1,0:T(8,128)(2,1)} %param.35) | copy-start | bytes 3145732
  28.1 69.4 %reduce-scatter.5.cloned.1.call-start = ((), (), s32[]{:S(2)}) async-start(), calls=%async_computation.5 | async-start | bytes 6291456 | tf_op jit(solution)/shard_map/reduce_scatter | solution.py:141
  76.3 7.8 %copy-start.3 = (bf16[2,512,8,64]{1,3,2,0:T(8,128)(2,1)}, bf16[2,512,8,64]{1,3,2,0:T(8,128)(2,1)S(1)}, u32[]{:S(2)}) copy-start(bf16[2,512,8,64]{1,3,2,0:T(8,128)(2,1)S(1)} %get-tuple-element.399) | copy-start | bytes 3145732
  76.3 7.8 %copy-start.5 = (bf16[2,512,8,64]{1,3,2,0:T(8,128)(2,1)}, bf16[2,512,8,64]{1,3,2,0:T(8,128)(2,1)S(1)}, u32[]{:S(2)}) copy-start(bf16[2,512,8,64]{1,3,2,0:T(8,128)(2,1)S(1)} %get-tuple-element.400) | copy-start | bytes 3145732
  76.3 7.8 %copy-start.7 = (bf16[2,512,8,64]{1,3,2,0:T(8,128)(2,1)}, bf16[2,512,8,64]{1,3,2,0:T(8,128)(2,1)S(1)}, u32[]{:S(2)}) copy-start(bf16[2,512,8,64]{1,3,2,0:T(8,128)(2,1)S(1)} %get-tuple-element.401) | copy-start | bytes 3145732
  76.3 7.8 %copy-start.37 = (f32[2,8,512]{2,1,0:T(8,128)}, f32[2,8,512]{2,1,0:T(8,128)S(1)}, u32[]{:S(2)}) copy-start(f32[2,8,512]{2,1,0:T(8,128)S(1)} %get-tuple-element.355) | copy-start | bytes 98308
  76.3 4.4 copy-start.35
  80.8 3.9 copy-start.44
  80.8 4.0 copy-start.45
  80.8 4.0 copy-start.46
  84.1 29.7 %all-gather.7.cloned.1.call-start = ((), (), s32[]{:S(2)}) async-start(), calls=%async_computation.6 | async-start | bytes 3145728 | tf_op jit(solution)/shard_map/all_gather | solution.py:152
  101.8 58.7 %reduce-scatter.7.cloned.1.call-start = ((), (), s32[]{:S(2)}) async-start(), calls=%async_computation.7 | async-start | bytes 6291456 | tf_op jit(solution)/shard_map/reduce_scatter | solution.py:155
  113.8 27.3 %copy-start.52 = (bf16[2048,1024]{1,0:T(8,128)(2,1)S(1)}, bf16[2048,1024]{1,0:T(8,128)(2,1)}, u32[]{:S(2)}) copy-start(bf16[2048,1024]{1,0:T(8,128)(2,1)} %param.43) | copy-start | bytes 12582916
  147.1 34.6 %all-gather.9.cloned.1.call-start = ((), (), s32[]{:S(2)}) async-start(), calls=%async_computation.8 | async-start | bytes 3145728 | tf_op jit(solution)/shard_map/all_gather | solution.py:172
  147.8 15.4 %copy-start.24 = (bf16[512,1024]{1,0:T(8,128)(2,1)S(1)}, bf16[512,1024]{1,0:T(8,128)(2,1)}, u32[]{:S(2)}) copy-start(bf16[512,1024]{1,0:T(8,128)(2,1)} %param.47) | copy-start | bytes 3145732
  169.7 45.0 %reduce-scatter.9.cloned.1.call-start = ((), (), s32[]{:S(2)}) async-start(), calls=%async_computation.9 | async-start | bytes 6291456 | tf_op jit(solution)/shard_map/reduce_scatter | solution.py:177
  181.7 13.5 %copy-start.53 = (bf16[1024,2048]{1,0:T(8,128)(2,1)S(1)}, bf16[1024,2048]{1,0:T(8,128)(2,1)}, u32[]{:S(2)}) copy-start(bf16[1024,2048]{1,0:T(8,128)(2,1)} %param.41) | copy-start | bytes 12582916
  201.3 31.7 %all-gather.11.cloned.1.call-start = ((), (), s32[]{:S(2)}) async-start(), calls=%async_computation.10 | async-start | bytes 3145728 | tf_op jit(solution)/shard_map/all_gather | solution.py:183
  217.8 15.2 %copy-start.36 = (bf16[512,1024]{1,0:T(8,128)(2,1)S(1)}, bf16[512,1024]{1,0:T(8,128)(2,1)}, u32[]{:S(2)}) copy-start(bf16[512,1024]{1,0:T(8,128)(2,1)} %param.37) | copy-start | bytes 3145732
  221.0 180.1 %reduce-scatter.11.cloned.1.call-start = ((), (), s32[]{:S(2)}) async-start(), calls=%async_computation.11 | async-start | bytes 3145728 | tf_op jit(solution)/shard_map/reduce_scatter | solution.py:195
  236.8 10.6 %copy-start.4 = (bf16[2,512,8,64]{1,3,2,0:T(8,128)(2,1)S(1)}, bf16[2,512,8,64]{1,3,2,0:T(8,128)(2,1)}, u32[]{:S(2)}) copy-start(bf16[2,512,8,64]{1,3,2,0:T(8,128)(2,1)} %copy-done.3) | copy-start | bytes 3145732
  236.8 10.6 %copy-start.6 = (bf16[2,512,8,64]{1,3,2,0:T(8,128)(2,1)S(1)}, bf16[2,512,8,64]{1,3,2,0:T(8,128)(2,1)}, u32[]{:S(2)}) copy-start(bf16[2,512,8,64]{1,3,2,0:T(8,128)(2,1)} %copy-done.5) | copy-start | bytes 3145732
  236.8 10.6 %copy-start.8 = (bf16[2,512,8,64]{1,3,2,0:T(8,128)(2,1)S(1)}, bf16[2,512,8,64]{1,3,2,0:T(8,128)(2,1)}, u32[]{:S(2)}) copy-start(bf16[2,512,8,64]{1,3,2,0:T(8,128)(2,1)} %copy-done.7) | copy-start | bytes 3145732
  236.8 10.6 %copy-start.38 = (f32[2,8,512]{2,1,0:T(8,128)S(1)}, f32[2,8,512]{2,1,0:T(8,128)}, u32[]{:S(2)}) copy-start(f32[2,8,512]{2,1,0:T(8,128)} %copy-done.37) | copy-start | bytes 98308
  251.1 2.6 copy-start.19
  262.9 2.6 copy-start.19
  271.3 2.7 copy-start.21
  271.3 4.1 copy-start.15
  274.1 2.7 copy-start.57
  275.4 2.7 copy-start.31
  282.4 393.2 %all-reduce.5.cloned.1.call-start = ((), (), s32[]{:S(2)}) async-start(), calls=%async_computation.12 | async-start | bytes 25165824 | tf_op jit(solution)/shard_map/psum | solution.py:216
  282.9 9.5 %copy-start.55 = (bf16[1024,1024]{1,0:T(8,128)(2,1)S(1)}, bf16[1024,1024]{1,0:T(8,128)(2,1)}, u32[]{:S(2)}) copy-start(bf16[1024,1024]{1,0:T(8,128)(2,1)} %all-gather.7.cloned.1.call-done) | copy-start | bytes 6291460
  283.0 9.5 %copy-start.60 = (bf16[1024,2048]{1,0:T(8,128)(2,1)S(1)}, bf16[1024,2048]{1,0:T(8,128)(2,1)}, u32[]{:S(2)}) copy-start(bf16[1024,2048]{1,0:T(8,128)(2,1)} %copy-done.59) | copy-start | bytes 12582916
  292.5 6.3 copy-start.17
  292.5 6.3 copy-start.56
  307.9 47.3 %copy-start.43 = (bf16[2048]{0:T(1024)(128)(2,1)S(1)}, bf16[2048]{0:T(1024)(128)(2,1)}, u32[]{:S(2)}) copy-start(bf16[2048]{0:T(1024)(128)(2,1)} %get-tuple-element.214) | copy-start | bytes 12292
  307.9 93.1 %copy-start.11 = (f32[512,1024]{1,0:T(8,128)S(1)}, f32[512,1024]{1,0:T(8,128)}, u32[]{:S(2)}) copy-start(f32[512,1024]{1,0:T(8,128)} %copy-done.10) | copy-start | bytes 6291460
  675.7 6.8 copy-start.18
  682.5 4.4 copy-start.30
  682.5 6.1 copy-start.29
  686.9 3.2 copy-start.28
  686.9 4.8 copy-start.27
  688.5 4.8 copy-start.1
  (30 other events, 40.7 us)
Sparse Core Ops, SparseCore 0:
  28.2 13.2 all-gather.4
  84.3 13.1 reduce-scatter.4
  101.9 11.8 all-gather.6
  147.2 13.2 reduce-scatter.6
  169.8 11.8 all-gather.8
  201.4 13.2 reduce-scatter.8
  221.1 11.8 all-gather.10
  282.6 10.7 reduce-scatter.10
  308.1 367.5 all-reduce.4
where the time goes:
time: 706 us; the launch traced here: 700 us
  waiting for transfers between devices  359 us (51%)
  matrix products  117 us (17%)
  blocking collectives  88.8 us (13%)
  local copies, waits for them, and re-layouts  64.2 us (9%)
  other arithmetic  53.5 us (8%)
  between operations  14.7 us (2%)
    psum x1, waiting for transfers between devices, shards(): lax.psum(grad_w_query.astype(jnp.bfloat16), 'batch').astype(jnp.float32)  272 us
    psum x1, blocking collectives, shards(): lax.psum((grad_b_out, grad_ln1_gain, grad_ln1_bias, grad_b_down, grad_ln2...  44.8 us
    psum x1, blocking collectives, shards(): lax.psum(grad_b_query.astype(jnp.bfloat16), 'batch').astype(jnp.float32)  44 us
    dot_general x6, matrix products, contract_last(): lax.dot_general(left, right, (((1,), (1,)), ((), ())), preferred_element_...  26.7 us
    dot_general x1, matrix products, shards(): jnp.dot(mid_all, w_up, preferred_element_type=jnp.float32)  25.3 us
    dot_general x6, matrix products, contract_rows(): lax.dot_general(left, right, (((0,), (0,)), ((), ())), preferred_element_...  24.9 us
  transfers between devices with their start and end apart: 9, of which 8 were waited for; matrix products, arithmetic and copies ran while one was open for 5% of the time, Pallas kernels for 0%

commit v1 on v0

--- a/solution.py
+++ b/solution.py
@@ -6,6 +6,11 @@
 HDIM = 64
 PAGE_LEN = 512
 CELLS = 128
+
+
+def add_all(x, axis):
+    parts = lax.all_gather(x, axis)
+    return jnp.sum(parts, axis=0)
 
 
 def contract_rows(left, right):
@@ -213,7 +218,7 @@
         grad_b_up,
         grad_w_down,
     ) = (
-        lax.psum(grad_w_query.astype(jnp.bfloat16), "batch").astype(jnp.float32),
+        add_all(grad_w_query.astype(jnp.bfloat16), "batch").astype(jnp.float32),
         lax.psum(grad_b_query.astype(jnp.bfloat16), "batch").astype(jnp.float32),
         lax.psum(grad_w_key.astype(jnp.bfloat16), "batch").astype(jnp.float32),
         lax.psum(grad_w_value.astype(jnp.bfloat16), "batch").astype(jnp.float32),

time: 706 us -> 864 us (1.22)
  waiting for transfers between devices: 359 us -> 507 us
  other arithmetic: 53.5 us -> 63.1 us
    all_gather x0 -> x1, waiting for transfers between devices: none -> 176 us  [add_all(): parts = lax.all_gather(x, axis)]
    psum x1, waiting for transfers between devices: 272 us -> 243 us  [shards(): lax.psum(grad_w_key.astype(jnp.bfloat16), 'batch').astype(jnp.float32)]
    reduce_sum x0 -> x1, other arithmetic: none -> 9.04 us  [add_all(): return jnp.sum(parts, axis=0)]
  transfers between devices with their start and end apart: 9 -> 10, of which waited for: 8 -> 9; matrix products, arithmetic and copies ran while one was open for 5% -> 6% of each run, Pallas kernels for 0% -> 0%
where the time goes in v1:
time: 864 us; the launch traced here: 858 us
  waiting for transfers between devices  507 us (59%)
  matrix products  118 us (14%)
  blocking collectives  89.4 us (10%)
  local copies, waits for them, and re-layouts  64.3 us (7%)
  other arithmetic  63.1 us (7%)
  between operations  15.1 us (2%)
    psum x1, waiting for transfers between devices, shards(): lax.psum(grad_w_key.astype(jnp.bfloat16), 'batch').astype(jnp.float32)  243 us
    all_gather x1, waiting for transfers between devices, add_all(): parts = lax.all_gather(x, axis)  176 us
    psum x1, blocking collectives, shards(): lax.psum(grad_b_query.astype(jnp.bfloat16), 'batch').astype(jnp.float32)  45.1 us
    psum x1, blocking collectives, shards(): lax.psum((grad_b_out, grad_ln1_gain, grad_ln1_bias, grad_b_down, grad_ln2...  44.3 us
    dot_general x6, matrix products, contract_rows(): lax.dot_general(left, right, (((0,), (0,)), ((), ())), preferred_element_...  26.9 us
    dot_general x6, matrix products, contract_last(): lax.dot_general(left, right, (((1,), (1,)), ((), ())), preferred_element_...  26.7 us
    dot_general x1, matrix products, shards(): jnp.dot(mid_all, w_up, preferred_element_type=jnp.float32)  25.3 us
  transfers between devices with their start and end apart: 10, of which 9 were waited for; matrix products, arithmetic and copies ran while one was open for 6% of the time, Pallas kernels for 0%

profile of v1, /device:TPU:0, one launch (start us, length us, event | category | flops | bytes accessed | tf_op | source)
XLA Modules:
  0.0 858.5 jit_solution(6982019583735948537)
XLA Ops:
  13.0 2.8 gather_fusion.3
  15.7 5.5 gather_fusion.2
  21.2 2.8 gather_fusion.4
  24.0 4.1 fusion.92
  28.2 13.3 %all-gather.7.cloned.1.call-done = bf16[1024,1024]{1,0:T(8,128)(2,1)} async-done(((bf16[512,1024]{1,0:T(8,128)(2,1)}), bf16[1024,1024]{1,0:T(8,128)(2,1)}) %all-gather.7.cloned.1.call-update) | async-done | bytes 2097168 | tf_op jit(solution)/shard_map/all_gather | solution.py:130
  41.5 2.8 add_convert_fusion.3
  46.7 2.5 copy.58
  49.2 3.1 add_convert_fusion.2
  54.4 2.5 copy.59
  56.9 3.1 convolution_convert_fusion.7
  62.1 2.5 copy.60
  65.7 10.6 %while.26 = (s32[]{:T(128)}, bf16[2,512,8,64]{1,3,2,0:T(8,128)(2,1)}, f32[2,8,512]{2,1,0:T(8,128)S(1)}, bf16[2,512,8,64]{1,3,2,0:T(8,128)(2,1)S(1)}, bf16[2,512,...) while((s32[]{:T(128)}, bf16[2,512,8,64]{1,3,2,0:T(8,128)(2,1)}, ...), condition=%wide.region_3.5_spmd, body=%wide.region_0.4_spmd.sunk | while | flops 553906176 | bytes 35784848 | solution.py:144
  76.3 3.2 copy.61
  80.8 3.3 fusion.94
  84.8 12.7 %reduce-scatter.5.cloned.1.call-done = f32[512,1024]{1,0:T(8,128)} async-done(((f32[1024,1024]{1,0:T(8,128)}), f32[512,1024]{1,0:T(8,128)}) %reduce-scatter.5.cloned.1.call-update) | async-done | bytes 2097168 | tf_op jit(solution)/shard_map/reduce_scatter | solution.py:146
  97.5 2.5 fusion.91
  101.9 11.9 %all-gather.9.cloned.1.call-done = bf16[1024,1024]{1,0:T(8,128)(2,1)} async-done(((bf16[512,1024]{1,0:T(8,128)(2,1)}), bf16[1024,1024]{1,0:T(8,128)(2,1)}) %all-gather.9.cloned.1.call-update) | async-done | bytes 2097168 | tf_op jit(solution)/shard_map/all_gather | solution.py:157
  113.9 25.3 %fusion.60 = (bf16[1024,2048]{1,0:T(8,128)(2,1)S(1)}, f32[1024,2048]{1,0:T(8,128)}) fusion(f32[2048]{0:T(1024)S(1)} %convert_element_type.187, bf16[1024,1024]{1,0:T(8,128)(2,1)} %all-gather.9.cloned.1.call-done, bf16[1024,2048]{1,0:T(8,128)(2,1)} %param.41), kind=kOutput, calls=%fused_computation.71 | convolution fusion | flops 4433379328 | bytes 18882560 | tf_op jit(solution)/shard_map/dot_general | solution.py:158
  141.1 6.0 fusion.95
  147.8 12.7 %reduce-scatter.7.cloned.1.call-done = f32[512,1024]{1,0:T(8,128)} async-done(((f32[1024,1024]{1,0:T(8,128)}), f32[512,1024]{1,0:T(8,128)}) %reduce-scatter.7.cloned.1.call-update) | async-done | bytes 2097168 | tf_op jit(solution)/shard_map/reduce_scatter | solution.py:160
  164.8 2.4 fusion.87
  169.9 11.8 %all-gather.11.cloned.1.call-done = bf16[1024,1024]{1,0:T(8,128)(2,1)} async-done(((bf16[512,1024]{1,0:T(8,128)(2,1)}), bf16[1024,1024]{1,0:T(8,128)(2,1)}) %all-gather.11.cloned.1.call-update) | async-done | bytes 2097168 | tf_op jit(solution)/shard_map/all_gather | solution.py:177
  181.7 11.5 %fusion.93 = (bf16[2048]{0:T(1024)(128)(2,1)}, bf16[1024,2048]{1,0:T(8,128)(2,1)S(1)}) fusion(f32[1024,2048]{1,0:T(8,128)} %get-tuple-element.212, f32[2048]{0:T(1024)S(1)} %convert_element_type.187, bf16[1024,1024]{1,0:T(8,128)(2,1)} %all-gather.11.cloned.1.call-done, bf16[2048,1024]{1,0:T(8,128)(2,1)} %param.43), kind=kOutput, calls=%fused_computation.173 | convolution fusion | flops 4320131072 | bytes 18886656 | tf_op jit(solution)/shard_map/dot_general | solution.py:23
  195.2 6.1 fusion.96
  201.3 13.3 %reduce-scatter.9.cloned.1.call-done = f32[512,1024]{1,0:T(8,128)} async-done(((f32[1024,1024]{1,0:T(8,128)}), f32[512,1024]{1,0:T(8,128)}) %reduce-scatter.9.cloned.1.call-update) | async-done | bytes 2097168 | tf_op jit(solution)/shard_map/reduce_scatter | solution.py:182
  214.6 3.2 multiply_reduce_fusion.2
  221.2 11.8 %all-gather.13.cloned.1.call-done = bf16[1024,1024]{1,0:T(8,128)(2,1)} async-done(((bf16[512,1024]{1,0:T(8,128)(2,1)}), bf16[1024,1024]{1,0:T(8,128)(2,1)}) %all-gather.13.cloned.1.call-update) | async-done | bytes 2097168 | tf_op jit(solution)/shard_map/all_gather | solution.py:188
  233.0 3.8 convolution_convert_fusion.6
  236.9 4.0 reshape.218
  240.9 3.3 copy.65
  247.4 23.0 %while.27 = (s32[]{:T(128)}, bf16[2,512,8,64]{1,3,2,0:T(8,128)(2,1)}, bf16[2,512,8,64]{1,3,2,0:T(8,128)(2,1)}, bf16[2,512,8,64]{1,3,2,0:T(8,128)(2,1)}, bf16[2,5...) while((s32[]{:T(128)}, ...), condition=%wide.region_17.19_spmd, body=%wide.region_15.18_spmd.sunk | while | flops 1368649728 | bytes 97637696 | solution.py:191
  252.9 2.6 multiply_convert_fusion.2
  264.3 2.6 multiply_convert_fusion.2
  270.5 2.5 copy.68
  278.9 2.7 add_convert_fusion
  282.1 9.5 %convolution_convert_fusion = bf16[2048,1024]{1,0:T(8,128)(2,1)} fusion(bf16[1024,2048]{1,0:T(8,128)(2,1)} %copy-done.60, bf16[1024,1024]{1,0:T(8,128)(2,1)} %all-gather.11.cloned.1.call-done), kind=kOutput, calls=%fused_computation.94 | convolution fusion | flops 4297064448 | bytes 10485760 | tf_op jit(solution)/shard_map/dot_general | solution.py:17
  291.7 6.2 convolution_convert_fusion.1
  304.9 4.3 convolution_convert_fusion.5
  309.2 44.3 %all-reduce = (f32[1024]{0:T(1024)}, f32[1024]{0:T(1024)}, f32[1024]{0:T(1024)}, f32[1024]{0:T(1024)}, f32[1024]{0:T(1024)}, /*index=5*/f32[1024]{0:T(1024)}) all-reduce(f32[1024]{0:T(1024)S(1)} %get-tuple-element.195, f32[1024]{0:T(1024)S(1)} %get-tuple-element.135, ...), channel_id=1, replica_groups=mesh['batch'=16,'mp'=2] {'batch','mp'}, use_global_device_ids=true, to_apply=%region_28.30 | all-reduce | flops 6144 | bytes 49152 | tf_op jit(solution)/shard_map/psum | solution.py:231
  355.4 45.1 %all-reduce.1 = (bf16[512]{0:T(512)(128)(2,1)S(1)}, bf16[512]{0:T(512)(128)(2,1)S(1)}, bf16[2048]{0:T(1024)(128)(2,1)S(1)}) all-reduce(bf16[512]{0:T(512)(128)(2,1)S(1)} %reduce_sum.206, bf16[512]{0:T(512)(128)(2,1)S(1)} %reduce_sum.208, bf16[2048]{0:T(1024)(128)(2,1)S(1)} %copy-done.42), channel_id=1, replica_groups=mesh['batch'=16,'mp'=2] {'batch'}, use_global_device_ids=true, to_apply=%region_21.23 | all-reduce | flops 3072 | bytes 12288 | tf_op jit(solution)/shard_map/psum | solution.py:222
  402.3 3.0 convert_add_fusion
  405.3 242.7 %all-reduce.5.cloned.1.call-done = (bf16[1024,512]{1,0:T(8,128)(2,1)}, bf16[1024,512]{1,0:T(8,128)(2,1)}, bf16[512,1024]{1,0:T(8,128)(2,1)}, bf16[1024,2048]{1,0:T(8,128)(2,1)}, bf16[2048,1024]{1,0:T(8,128)(2,1)}) async-done(((bf16[1024,512]{1,0:T(8,128)(2,1)}, bf16[1024,512]{1,0:T(8,128)(2,1)}, bf16[512,1024]{1,0:T(8,128)(2,1)}, bf16[1024,2048]{1,0:T(8,128)(2,1)}, bf16[2048,1024]{1,0:T(8,128)(2,1)}), ...) | async-done | bytes 11534352 | tf_op jit(solution)/shard_map/psum | solution.py:223
  648.0 3.0 convert_element_type.204
  651.0 2.8 convert_element_type.206
  655.4 4.8 convert_element_type.211
  660.2 4.4 convert_element_type.214
  664.7 176.1 %all-gather.15.cloned.1.call-done = bf16[16384,512]{1,0:T(8,128)(2,1)} async-done(((bf16[1024,512]{1,0:T(8,128)(2,1)}), bf16[16384,512]{1,0:T(8,128)(2,1)}) %all-gather.15.cloned.1.call-update) | async-done | bytes 16777232 | tf_op jit(solution)/shard_map/all_gather | solution.py:12
  840.8 9.0 %reduce_sum.204 = bf16[1024,512]{1,0:T(8,128)(2,1)S(1)} reduce(bf16[16,1024,512]{2,1,0:T(8,128)(2,1)} %bitcast.162, bf16[]{:T(256)} %constant.89.clone.1), dimensions={0}, to_apply=%region_19.21 | reduce | flops 7864320 | bytes 17825794 | tf_op jit(solution)/shard_map/reduce_sum | solution.py:13
  (250 shorter events, 83.3 us)
Async XLA Ops:
  7.2 3.7 copy-start
  7.2 34.3 %all-gather.7.cloned.1.call-start = ((), (), s32[]{:S(2)}) async-start(), calls=%async_computation.4 | async-start | bytes 3145728 | tf_op jit(solution)/shard_map/all_gather | solution.py:130
  15.7 5.5 copy-start.2
  24.0 4.2 copy-start.49
  24.0 4.2 copy-start.50
  24.0 17.5 %copy-start.28 = (bf16[1024,512]{1,0:T(8,128)(2,1)S(1)}, bf16[1024,512]{1,0:T(8,128)(2,1)}, u32[]{:S(2)}) copy-start(bf16[1024,512]{1,0:T(8,128)(2,1)} %param.35) | copy-start | bytes 3145732
  28.1 69.5 %reduce-scatter.5.cloned.1.call-start = ((), (), s32[]{:S(2)}) async-start(), calls=%async_computation.5 | async-start | bytes 6291456 | tf_op jit(solution)/shard_map/reduce_scatter | solution.py:146
  76.3 7.8 copy-start.3
  76.3 7.8 copy-start.5
  76.3 7.8 copy-start.7
  76.3 7.8 copy-start.36
  76.3 4.5 copy-start.34
  80.8 3.9 copy-start.43
  80.8 4.0 copy-start.44
  80.8 4.0 copy-start.45
  84.2 29.7 %all-gather.9.cloned.1.call-start = ((), (), s32[]{:S(2)}) async-start(), calls=%async_computation.6 | async-start | bytes 3145728 | tf_op jit(solution)/shard_map/all_gather | solution.py:157
  101.9 58.7 %reduce-scatter.7.cloned.1.call-start = ((), (), s32[]{:S(2)}) async-start(), calls=%async_computation.7 | async-start | bytes 6291456 | tf_op jit(solution)/shard_map/reduce_scatter | solution.py:160
  113.9 27.2 %copy-start.51 = (bf16[2048,1024]{1,0:T(8,128)(2,1)S(1)}, bf16[2048,1024]{1,0:T(8,128)(2,1)}, u32[]{:S(2)}) copy-start(bf16[2048,1024]{1,0:T(8,128)(2,1)} %param.43) | copy-start | bytes 12582916
  147.2 34.6 %all-gather.11.cloned.1.call-start = ((), (), s32[]{:S(2)}) async-start(), calls=%async_computation.8 | async-start | bytes 3145728 | tf_op jit(solution)/shard_map/all_gather | solution.py:177
  147.8 15.4 %copy-start.27 = (bf16[512,1024]{1,0:T(8,128)(2,1)S(1)}, bf16[512,1024]{1,0:T(8,128)(2,1)}, u32[]{:S(2)}) copy-start(bf16[512,1024]{1,0:T(8,128)(2,1)} %param.47) | copy-start | bytes 3145732
  169.7 44.9 %reduce-scatter.9.cloned.1.call-start = ((), (), s32[]{:S(2)}) async-start(), calls=%async_computation.9 | async-start | bytes 6291456 | tf_op jit(solution)/shard_map/reduce_scatter | solution.py:182
  181.7 13.5 %copy-start.52 = (bf16[1024,2048]{1,0:T(8,128)(2,1)S(1)}, bf16[1024,2048]{1,0:T(8,128)(2,1)}, u32[]{:S(2)}) copy-start(bf16[1024,2048]{1,0:T(8,128)(2,1)} %param.41) | copy-start | bytes 12582916
  201.3 31.7 %all-gather.13.cloned.1.call-start = ((), (), s32[]{:S(2)}) async-start(), calls=%async_computation.10 | async-start | bytes 3145728 | tf_op jit(solution)/shard_map/all_gather | solution.py:188
  217.8 15.2 %copy-start.35 = (bf16[512,1024]{1,0:T(8,128)(2,1)S(1)}, bf16[512,1024]{1,0:T(8,128)(2,1)}, u32[]{:S(2)}) copy-start(bf16[512,1024]{1,0:T(8,128)(2,1)} %param.37) | copy-start | bytes 3145732
  221.0 181.3 %reduce-scatter.11.cloned.1.call-start = ((), (), s32[]{:S(2)}) async-start(), calls=%async_computation.11 | async-start | bytes 3145728 | tf_op jit(solution)/shard_map/reduce_scatter | solution.py:200
  236.8 10.6 %copy-start.4 = (bf16[2,512,8,64]{1,3,2,0:T(8,128)(2,1)S(1)}, bf16[2,512,8,64]{1,3,2,0:T(8,128)(2,1)}, u32[]{:S(2)}) copy-start(bf16[2,512,8,64]{1,3,2,0:T(8,128)(2,1)} %copy-done.3) | copy-start | bytes 3145732
  236.8 10.6 %copy-start.6 = (bf16[2,512,8,64]{1,3,2,0:T(8,128)(2,1)S(1)}, bf16[2,512,8,64]{1,3,2,0:T(8,128)(2,1)}, u32[]{:S(2)}) copy-start(bf16[2,512,8,64]{1,3,2,0:T(8,128)(2,1)} %copy-done.5) | copy-start | bytes 3145732
  236.8 10.6 %copy-start.8 = (bf16[2,512,8,64]{1,3,2,0:T(8,128)(2,1)S(1)}, bf16[2,512,8,64]{1,3,2,0:T(8,128)(2,1)}, u32[]{:S(2)}) copy-start(bf16[2,512,8,64]{1,3,2,0:T(8,128)(2,1)} %copy-done.7) | copy-start | bytes 3145732
  236.8 10.6 %copy-start.37 = (f32[2,8,512]{2,1,0:T(8,128)S(1)}, f32[2,8,512]{2,1,0:T(8,128)}, u32[]{:S(2)}) copy-start(f32[2,8,512]{2,1,0:T(8,128)} %copy-done.36) | copy-start | bytes 98308
  270.5 2.7 copy-start.15
  270.5 4.1 copy-start.18
  273.2 2.7 copy-start.32
  273.2 2.7 copy-start.56
  281.6 366.4 %all-reduce.5.cloned.1.call-start = ((), (), s32[]{:S(2)}) async-start(), calls=%async_computation.13 | async-start | bytes 23068672 | tf_op jit(solution)/shard_map/psum | solution.py:223
  282.1 9.5 %copy-start.54 = (bf16[1024,1024]{1,0:T(8,128)(2,1)S(1)}, bf16[1024,1024]{1,0:T(8,128)(2,1)}, u32[]{:S(2)}) copy-start(bf16[1024,1024]{1,0:T(8,128)(2,1)} %all-gather.9.cloned.1.call-done) | copy-start | bytes 6291460
  282.1 9.5 %copy-start.59 = (bf16[1024,2048]{1,0:T(8,128)(2,1)S(1)}, bf16[1024,2048]{1,0:T(8,128)(2,1)}, u32[]{:S(2)}) copy-start(bf16[1024,2048]{1,0:T(8,128)(2,1)} %copy-done.58) | copy-start | bytes 12582916
  291.6 6.3 copy-start.20
  291.7 6.3 copy-start.55
  304.8 4.4 copy-start.38
  304.8 4.4 copy-start.39
  304.8 4.4 copy-start.40
  304.8 50.6 %copy-start.42 = (bf16[2048]{0:T(1024)(128)(2,1)S(1)}, bf16[2048]{0:T(1024)(128)(2,1)}, u32[]{:S(2)}) copy-start(bf16[2048]{0:T(1024)(128)(2,1)} %get-tuple-element.213) | copy-start | bytes 12292
  304.8 97.4 %copy-start.11 = (f32[512,1024]{1,0:T(8,128)S(1)}, f32[512,1024]{1,0:T(8,128)}, u32[]{:S(2)}) copy-start(f32[512,1024]{1,0:T(8,128)} %copy-done.10) | copy-start | bytes 6291460
  304.8 535.9 %all-gather.15.cloned.1.call-start = ((), (), s32[]{:S(2)}) async-start(), calls=%async_computation.12 | async-start | bytes 17825792 | tf_op jit(solution)/shard_map/all_gather | solution.py:12
  648.0 5.8 copy-start.30
  648.0 7.4 copy-start.22
  655.4 4.8 copy-start.21
  840.8 10.7 %copy-start.1 = (bf16[1024,1024]{1,0:T(8,128)(2,1)S(1)}, bf16[1024,1024]{1,0:T(8,128)(2,1)}, u32[]{:S(2)}) copy-start(bf16[1024,1024]{1,0:T(8,128)(2,1)} %param.30) | copy-start | bytes 6291460
  (32 other events, 47.5 us)
Sparse Core Ops, SparseCore 0:
  28.2 13.2 all-gather.6
  84.3 13.2 reduce-scatter.4
  102.0 11.8 all-gather.8
  147.3 13.1 reduce-scatter.6
  169.8 11.8 all-gather.10
  201.4 13.1 reduce-scatter.8
  221.1 11.8 all-gather.12
  281.7 10.7 reduce-scatter.10
  304.9 343.0 all-reduce.4
  650.6 190.1 all-gather.14
